TPU v7x, 512 devices: a whole 4x8x8 slice. The times are simulated.
512 devices in a mesh: section: 4 (over x), sub: 32 (over z_lo, y), rng: 4 (over z_hi, core).
Axes of the slice: x: 4, y: 8, z: 8 (z_hi: 2, z_lo: 4; z = z_hi * 4 + z_lo), core: 2. Of those that a mesh axis runs over, the one named last changes fastest.
Arguments:
- echoes: bfloat16 [2, 32, 24, 16384], P(None, 'sub', 'section', 'rng'), may hold values from -6 to 6
- chirp: bfloat16 [2, 2048], replicated, may hold values from -0.25 to 0.25
- steer: bfloat16 [2, 32, 128, 24], P(None, 'sub'), may hold values from -2 to 2
- pulse_order: int32 [32, 24], P('sub'), may hold values from 0 to 23, each once within a row
- band_coef: bfloat16 [5, 32, 2, 2, 128, 16], P(None, 'sub'), may hold values from -2.5 to 2.5
- band_start: int32 [5, 32, 2, 128], P(None, 'sub'), may hold values from 0 to 112
- band_width: int32 [5, 32, 2, 128], P(None, 'sub'), may hold values from 1 to 16
Outputs:
- image: bfloat16 [2, 4096, 4, 4096], P(None, 'sub', 'rng', 'section')
Inputs may be any that keep to these rules, and one draw needn't show every extreme that they name: `pulse_order`: each row is a permutation of the 24 aperture positions.
All inputs are finite; a program needn't handle non-finite values.
Results may differ from a plain program's by a relative error of at most 0.0085.
Values may be sent and summed in bfloat16 or wider, within the bound.
A program may use at most 64 MiB of HBM per device.

v0:
```python
import jax
import jax.numpy as jnp
from jax import lax
from jax.sharding import PartitionSpec as P

CBLK = 128


def from_behind(value, axis, by):
    size = lax.axis_size(axis)
    pairs = [(i, i + by) for i in range(size) if 0 <= i + by < size]
    return lax.ppermute(value, axis, pairs)


def from_partner(block, axis, stride):
    count = lax.axis_size(axis)
    route = []
    for low in range(count):
        high = low | 1 << stride
        if high != low and high < count:
            route += [(low, high), (high, low)]
    return lax.ppermute(block, axis, route)


def band_matrix(coef_side, start_side, width_side):
    beam_count = coef_side.shape[1]
    tap_count = coef_side.shape[2]
    column = jnp.arange(beam_count, dtype=jnp.int32)
    offset = column[None, :] - start_side[:, None]
    taps = jnp.arange(tap_count, dtype=jnp.int32)
    hits = (offset[None, :, :] == taps[:, None, None]) & (
        taps[:, None, None] < width_side[None, :, None]
    )
    selector = hits.astype(jnp.bfloat16)
    return jnp.einsum(
        "sqt,tqc->sqc", coef_side, selector, preferred_element_type=jnp.float32
    ).astype(jnp.bfloat16)


def merge_level(own, partner_image, coef_level, start_level, width_level):
    self_matrix = band_matrix(coef_level[0], start_level[0], width_level[0])
    cross_matrix = band_matrix(coef_level[1], start_level[1], width_level[1])
    upper_rows = jnp.concatenate(
        [self_matrix[0], -self_matrix[1], cross_matrix[0], -cross_matrix[1]], axis=1
    )
    lower_rows = jnp.concatenate(
        [self_matrix[1], self_matrix[0], cross_matrix[1], cross_matrix[0]], axis=1
    )
    operator = jnp.concatenate([upper_rows, lower_rows], axis=0)
    stacked = jnp.concatenate([own[0], own[1], partner_image[0], partner_image[1]], axis=0)
    merged = jnp.dot(operator, stacked, preferred_element_type=jnp.float32)
    return merged.reshape(2, own.shape[1], own.shape[2]).astype(jnp.bfloat16)


def lag_tables(chirp, extra_blocks):
    tap_count = chirp.shape[1]
    padded = jnp.concatenate(
        [jnp.zeros((2, CBLK), jnp.bfloat16), chirp, jnp.zeros((2, 2 * CBLK), jnp.bfloat16)], axis=1
    )
    total_len = tap_count + 3 * CBLK
    tiled = jnp.tile(padded, (1, CBLK))[:, : CBLK * (total_len - 1)]
    shifted = tiled.reshape(2, CBLK, total_len - 1)[:, :, CBLK : CBLK + (extra_blocks + 1) * CBLK]
    shifted = shifted.reshape(2, CBLK, extra_blocks + 1, CBLK)
    return jnp.transpose(shifted, (0, 2, 3, 1))


def compress(signal, chirp):
    pulse_count = signal.shape[1]
    range_count = signal.shape[2]
    tap_count = chirp.shape[1]
    next_rim = from_behind(signal[:, :, :tap_count], "rng", -1)
    extended = jnp.concatenate([signal, next_rim], axis=2)
    block_count = range_count // CBLK
    extra_blocks = tap_count // CBLK
    blocks = extended.reshape(2, pulse_count, block_count + extra_blocks, CBLK)
    blocks = jnp.transpose(blocks, (1, 2, 0, 3)).reshape(
        pulse_count, block_count + extra_blocks, 2 * CBLK
    )
    parts_table = lag_tables(chirp, extra_blocks)
    chirp_real = parts_table[0]
    chirp_imag = parts_table[1]
    upper_rows = jnp.concatenate([chirp_real, -chirp_imag], axis=2)
    lower_rows = jnp.concatenate([chirp_imag, chirp_real], axis=2)
    tables = jnp.concatenate([upper_rows, lower_rows], axis=1)

    def add_piece(lag, accumulated):
        window = lax.dynamic_slice_in_dim(blocks, lag, block_count, 1)
        table = lax.dynamic_index_in_dim(tables, lag, 0, keepdims=False)
        return accumulated + jnp.einsum(
            "pbi,io->pbo", window, table, preferred_element_type=jnp.float32
        )

    accumulated = lax.fori_loop(
        0, extra_blocks + 1, add_piece, jnp.zeros((pulse_count, block_count, 2 * CBLK), jnp.float32)
    )
    accumulated = accumulated.reshape(pulse_count, block_count, 2, CBLK)
    return (
        jnp.transpose(accumulated, (2, 0, 1, 3))
        .reshape(2, pulse_count, range_count)
        .astype(jnp.bfloat16)
    )


def on_device(echoes, chirp, steer, pulse_order, band_coef, band_start, band_width):
    compressed = compress(echoes[:, 0], chirp)
    pulse_rows = lax.all_to_all(compressed, "section", split_axis=2, concat_axis=1, tiled=True)
    position_count = pulse_order.shape[1]
    positions = jnp.arange(position_count, dtype=jnp.int32)
    selector = (positions[:, None] == pulse_order[0][None, :]).astype(jnp.bfloat16)
    weights = jnp.einsum(
        "sqj,jk->sqk", steer[:, 0], selector, preferred_element_type=jnp.float32
    ).astype(jnp.bfloat16)
    forming = jnp.concatenate(
        [
            jnp.concatenate([weights[0], -weights[1]], axis=1),
            jnp.concatenate([weights[1], weights[0]], axis=1),
        ],
        axis=0,
    )
    stacked_rows = jnp.concatenate([pulse_rows[0], pulse_rows[1]], axis=0)
    beam_count = weights.shape[1]
    level_image = (
        jnp.dot(forming, stacked_rows, preferred_element_type=jnp.float32)
        .reshape(2, beam_count, pulse_rows.shape[2])
        .astype(jnp.bfloat16)
    )
    bit_count = lax.axis_size("sub").bit_length() - 1
    coef_all = band_coef[:, 0]
    start_all = band_start[:, 0]
    width_all = band_width[:, 0]
    section_count = coef_all.shape[0]
    for level in range(section_count):
        partner_image = from_partner(level_image, "sub", level % bit_count)
        level_image = merge_level(
            level_image, partner_image, coef_all[level], start_all[level], width_all[level]
        )
    return level_image[:, :, None, :]


def solution(mesh):
    return jax.shard_map(
        on_device,
        mesh=mesh,
        in_specs=(
            P(None, "sub", "section", "rng"),
            P(),
            P(None, "sub", None, None),
            P("sub", None),
            P(None, "sub", None, None, None, None),
            P(None, "sub", None, None),
            P(None, "sub", None, None),
        ),
        out_specs=P(None, "sub", "rng", "section"),
        check_vma=False,
    )
```

profile of v0, /device:TPU:1, one launch (start us, length us, event | category | flops | bytes accessed | tf_op | source)
XLA Modules:
  0.0 180.4 jit_solution(6251457165325808575)
XLA Ops:
  0.0 1.5 slice.437
  1.5 8.8 %collective-permute-start = (bf16[2,6,2048]{2,0,1:T(2,128)(2,1)}, bf16[2,6,2048]{2,0,1:T(2,128)(2,1)}, u32[]{:S(2)}, u32[]{:S(2)}) collective-permute-start(bf16[2,6,2048]{2,0,1:T(2,128)(2,1)} %slice.437), channel_id=1, source_target_pairs={{1,0},{2,1},{3,2},{5,4},{6,5},{7,6},{9,8},{10,9},{11,10},{13,12},{... | collective-permute-start | bytes 147464 | tf_op jit(solution)/shard_map/ppermute | solution.py:12
  10.3 0.7 maximum_maximum_fusion.1
  11.1 1.3 copy.173
  12.4 0.9 slice.438
  13.3 2.1 %reshape.582 = bf16[622336]{0:T(1024)(128)(2,1)S(1)} reshape(bf16[2,311168]{1,0:T(2,128)(2,1)S(1)} %slice.438) | data formatting | bytes 2489344
  15.5 2.2 %reshape.578 = bf16[2,128,2431]{2,1,0:T(8,128)(2,1)S(1)} reshape(bf16[622336]{0:T(1024)(128)(2,1)S(1)} %reshape.582) | data formatting | bytes 2489344 | tf_op jit(solution)/shard_map/reshape | solution.py:62
  17.7 1.1 slice.439
  18.7 1.7 copy.133
  20.6 0.9 fusion.186
  21.5 0.5 slice_bitcast_fusion.33
  22.0 0.6 slice_bitcast_fusion.32
  22.6 0.6 fusion.198
  23.5 0.5 fusion.12
  24.1 0.6 fusion.195
  24.9 0.5 fusion.13
  25.3 0.7 fusion.208
  26.1 0.6 fusion.196
  26.9 0.6 slice_bitcast_fusion.12
  27.8 0.5 fusion.10
  28.4 0.6 fusion.193
  29.2 0.5 fusion.11
  29.6 0.7 fusion.206
  30.3 0.6 fusion.194
  31.3 0.5 fusion.8
  31.9 0.7 fusion.191
  32.7 0.5 fusion.9
  33.1 0.7 fusion.204
  33.8 0.6 fusion.192
  34.5 0.8 iota_subtract_fusion.6
  35.3 1.4 maximum_maximum_fusion
  36.7 1.1 maximum_bitcast_fusion
  37.9 4.0 %while.14 = (s32[]{:T(128)}, f32[6,32,256]{2,1,0:T(8,128)S(1)}, bf16[6,48,256]{2,1,0:T(8,128)(2,1)S(1)}, bf16[17,256,256]{2,1,0:T(8,128)(2,1)S(1)}, s32[]{:T(128)}, /*index=5*/s32[]{:T(128)}) while((s32[]{:T(128)}, f32[6,32,256]{2,1,0:T(8,128)S(1)}, bf16[6,48,256]{2,1,0:T(8,128)(2,1)S(1)}, bf16[17,256,256]{2,1,0:T(8,128)(2,1)S(1)}, ...), condition=%wide.region_1.2_spmd.clone, body=%wide.region_0.1_spmd.clone.sunk | while | flops 25264132 | bytes 623695 | solution.py:93
  37.9 0.2 convolution_add_fusion.2
  38.2 0.2 convolution_add_fusion.2
  38.6 0.2 convolution_add_fusion.2
  38.9 0.2 convolution_add_fusion.2
  39.1 0.2 convolution_add_fusion.2
  41.9 1.4 copy.140
  43.3 4.2 %reshape.584 = bf16[4,2,6144]{2,1,0:T(2,128)(2,1)} reshape(bf16[4096,2,6]{2,1,0:T(2,128)(2,1)S(1)} %bitcast.228) | data formatting | bytes 196608
  47.5 3.5 %all-to-all-start = ((bf16[4,2,6144]{2,1,0:T(2,128)(2,1)}), bf16[4,2,6144]{2,1,0:T(2,128)(2,1)S(1)}, u32[]{:S(2)}, u32[]{:S(2)}) async-start(bf16[4,2,6144]{2,1,0:T(2,128)(2,1)} %reshape.584), calls=%async_computation | async-start | bytes 196608 | tf_op jit(solution)/shard_map/all_to_all | solution.py:106
  51.0 4.9 %all-to-all-done = bf16[4,2,6144]{2,1,0:T(2,128)(2,1)S(1)} async-done(((bf16[4,2,6144]{2,1,0:T(2,128)(2,1)}), bf16[4,2,6144]{2,1,0:T(2,128)(2,1)S(1)}, u32[]{:S(2)}, u32[]{:S(2)}) %all-to-all-start) | async-done | bytes 98336 | tf_op jit(solution)/shard_map/all_to_all | solution.py:106
  55.9 4.8 %reshape.585 = bf16[4096,2,6]{2,1,0:T(2,128)(2,1)S(1)} reshape(bf16[4,2,6144]{2,1,0:T(2,128)(2,1)S(1)} %all-to-all-done) | data formatting | bytes 196608
  60.7 1.5 copy.141
  62.4 0.3 convolution_convert_fusion.5
  62.8 1.9 %collective-permute-start.1 = (bf16[2,128,1024]{2,1,0:T(8,128)(2,1)S(1)}, bf16[2,128,1024]{2,1,0:T(8,128)(2,1)S(1)}, u32[]{:S(2)}, u32[]{:S(2)}) collective-permute-start(bf16[2,128,1024]{2,1,0:T(8,128)(2,1)S(1)} %bitcast.233), channel_id=1, source_target_pairs={{0,4},{4,0},{8,12},{12,8},{16,20},{20,16},{24,28},{28,24},{32,36},... | collective-permute-start | bytes 1572872 | tf_op jit(solution)/shard_map/ppermute | solution.py:22
  65.0 0.5 fusion.6
  65.6 12.2 %collective-permute-done.1 = bf16[2,128,1024]{2,1,0:T(8,128)(2,1)S(1)} collective-permute-done((bf16[2,128,1024]{2,1,0:T(8,128)(2,1)S(1)}, bf16[2,128,1024]{2,1,0:T(8,128)(2,1)S(1)}, u32[]{:S(2)}, u32[]{:S(2)}) %collective-permute-start.1) | collective-permute-done | bytes 524320 | tf_op jit(solution)/shard_map/ppermute | solution.py:22
  77.9 0.4 convolution_convert_fusion.4
  78.4 2.1 %collective-permute-start.2 = (bf16[2,128,1024]{2,1,0:T(8,128)(2,1)S(1)}, bf16[2,128,1024]{2,1,0:T(8,128)(2,1)S(1)}, u32[]{:S(2)}, u32[]{:S(2)}) collective-permute-start(bf16[2,128,1024]{2,1,0:T(8,128)(2,1)S(1)} %bitcast.247), channel_id=1, source_target_pairs={{0,8},{8,0},{4,12},{12,4},{16,24},{24,16},{20,28},{28,20},{32,40},... | collective-permute-start | bytes 1572872 | tf_op jit(solution)/shard_map/ppermute | solution.py:22
  80.8 0.5 fusion.7
  81.2 25.1 %collective-permute-done.2 = bf16[2,128,1024]{2,1,0:T(8,128)(2,1)S(1)} collective-permute-done((bf16[2,128,1024]{2,1,0:T(8,128)(2,1)S(1)}, bf16[2,128,1024]{2,1,0:T(8,128)(2,1)S(1)}, u32[]{:S(2)}, u32[]{:S(2)}) %collective-permute-start.2) | collective-permute-done | bytes 524320 | tf_op jit(solution)/shard_map/ppermute | solution.py:22
  106.4 0.5 convolution_convert_fusion.3
  107.0 3.0 %collective-permute-start.3 = (bf16[2,128,1024]{2,1,0:T(8,128)(2,1)S(1)}, bf16[2,128,1024]{2,1,0:T(8,128)(2,1)S(1)}, u32[]{:S(2)}, u32[]{:S(2)}) collective-permute-start(bf16[2,128,1024]{2,1,0:T(8,128)(2,1)S(1)} %bitcast.248), channel_id=1, source_target_pairs={{0,16},{16,0},{4,20},{20,4},{8,24},{24,8},{12,28},{28,12},{32,48},... | collective-permute-start | bytes 1572872 | tf_op jit(solution)/shard_map/ppermute | solution.py:22
  110.3 0.5 fusion.4
  110.8 24.9 %collective-permute-done.3 = bf16[2,128,1024]{2,1,0:T(8,128)(2,1)S(1)} collective-permute-done((bf16[2,128,1024]{2,1,0:T(8,128)(2,1)S(1)}, bf16[2,128,1024]{2,1,0:T(8,128)(2,1)S(1)}, u32[]{:S(2)}, u32[]{:S(2)}) %collective-permute-start.3) | collective-permute-done | bytes 524320 | tf_op jit(solution)/shard_map/ppermute | solution.py:22
  135.8 0.4 convolution_convert_fusion.2
  136.2 1.9 %collective-permute-start.4 = (bf16[2,128,1024]{2,1,0:T(8,128)(2,1)S(1)}, bf16[2,128,1024]{2,1,0:T(8,128)(2,1)S(1)}, u32[]{:S(2)}, u32[]{:S(2)}) collective-permute-start(bf16[2,128,1024]{2,1,0:T(8,128)(2,1)S(1)} %bitcast.249), channel_id=1, source_target_pairs={{0,32},{32,0},{4,36},{36,4},{8,40},{40,8},{12,44},{44,12},{16,48},... | collective-permute-start | bytes 1572872 | tf_op jit(solution)/shard_map/ppermute | solution.py:22
  138.4 0.5 fusion.5
  138.9 11.9 %collective-permute-done.4 = bf16[2,128,1024]{2,1,0:T(8,128)(2,1)S(1)} collective-permute-done((bf16[2,128,1024]{2,1,0:T(8,128)(2,1)S(1)}, bf16[2,128,1024]{2,1,0:T(8,128)(2,1)S(1)}, u32[]{:S(2)}, u32[]{:S(2)}) %collective-permute-start.4) | collective-permute-done | bytes 524320 | tf_op jit(solution)/shard_map/ppermute | solution.py:22
  150.9 0.5 convolution_convert_fusion.1
  151.4 3.2 %collective-permute-start.5 = (bf16[2,128,1024]{2,1,0:T(8,128)(2,1)S(1)}, bf16[2,128,1024]{2,1,0:T(8,128)(2,1)S(1)}, u32[]{:S(2)}, u32[]{:S(2)}) collective-permute-start(bf16[2,128,1024]{2,1,0:T(8,128)(2,1)S(1)} %bitcast.250), channel_id=1, source_target_pairs={{0,64},{64,0},{4,68},{68,4},{8,72},{72,8},{12,76},{76,12},{16,80},... | collective-permute-start | bytes 1572872 | tf_op jit(solution)/shard_map/ppermute | solution.py:22
  154.8 24.4 %collective-permute-done.5 = bf16[2,128,1024]{2,1,0:T(8,128)(2,1)S(1)} collective-permute-done((bf16[2,128,1024]{2,1,0:T(8,128)(2,1)S(1)}, bf16[2,128,1024]{2,1,0:T(8,128)(2,1)S(1)}, u32[]{:S(2)}, u32[]{:S(2)}) %collective-permute-start.5) | collective-permute-done | bytes 524320 | tf_op jit(solution)/shard_map/ppermute | solution.py:22
  179.2 1.2 convolution_convert_fusion
  (144 shorter events, 6.4 us)
Async XLA Ops:
  0.0 26.7 %copy-start = (bf16[2,1,128,24]{2,3,1,0:T(8,128)(2,1)S(1)}, bf16[2,1,128,24]{2,3,1,0:T(8,128)(2,1)}, u32[]{:S(2)}) copy-start(bf16[2,1,128,24]{2,3,1,0:T(8,128)(2,1)} %param.11) | copy-start | bytes 36868
  1.5 35.3 %collective-permute-start = (bf16[2,6,2048]{2,0,1:T(2,128)(2,1)}, bf16[2,6,2048]{2,0,1:T(2,128)(2,1)}, u32[]{:S(2)}, u32[]{:S(2)}) collective-permute-start(bf16[2,6,2048]{2,0,1:T(2,128)(2,1)} %slice.437), channel_id=1, source_target_pairs={{1,0},{2,1},{3,2},{5,4},{6,5},{7,6},{9,8},{10,9},{11,10},{13,12},{... | collective-permute-start | bytes 147464 | tf_op jit(solution)/shard_map/ppermute | solution.py:12
  20.4 1.1 copy-start.27
  20.4 1.6 copy-start.28
  20.4 2.1 %copy-start.4 = (bf16[5,1,2,2,128,16]{4,5,3,2,1,0:T(8,128)(2,1)S(1)}, bf16[5,1,2,2,128,16]{4,5,3,2,1,0:T(8,128)(2,1)}, u32[]{:S(2)}) copy-start(bf16[5,1,2,2,128,16]{4,5,3,2,1,0:T(8,128)(2,1)} %param.13) | copy-start | bytes 245764
  21.5 5.2 %copy-start.34 = (s32[1,24]{1,0:T(1,128)S(1)}, s32[1,24]{1,0:T(1,128)}, u32[]{:S(2)}) copy-start(s32[1,24]{1,0:T(1,128)} %param.12) | copy-start | bytes 292
  26.9 4.2 %copy-start.23 = (bf16[2,128,24]{1,2,0:T(8,128)(2,1)}, bf16[2,128,24]{1,2,0:T(8,128)(2,1)S(1)}, u32[]{:S(2)}) copy-start(bf16[2,128,24]{1,2,0:T(8,128)(2,1)S(1)} %fusion.14) | copy-start | bytes 36868
  41.9 9.0 %copy-start.24 = (bf16[2,128,24]{1,2,0:T(8,128)(2,1)S(1)}, bf16[2,128,24]{1,2,0:T(8,128)(2,1)}, u32[]{:S(2)}) copy-start(bf16[2,128,24]{1,2,0:T(8,128)(2,1)} %copy-done.23) | copy-start | bytes 36868
  47.5 8.4 %all-to-all-start = ((bf16[4,2,6144]{2,1,0:T(2,128)(2,1)}), bf16[4,2,6144]{2,1,0:T(2,128)(2,1)S(1)}, u32[]{:S(2)}, u32[]{:S(2)}) async-start(bf16[4,2,6144]{2,1,0:T(2,128)(2,1)} %reshape.584), calls=%async_computation | async-start | bytes 196608 | tf_op jit(solution)/shard_map/all_to_all | solution.py:106
  51.0 11.4 %copy-start.25 = (bf16[128,24]{0,1:T(8,128)(2,1)S(1)}, bf16[128,24]{0,1:T(8,128)(2,1)}, u32[]{:S(2)}) copy-start(bf16[128,24]{0,1:T(8,128)(2,1)} %get-tuple-element.172) | copy-start | bytes 18436
  51.0 11.4 %copy-start.26 = (bf16[128,24]{0,1:T(8,128)(2,1)S(1)}, bf16[128,24]{0,1:T(8,128)(2,1)}, u32[]{:S(2)}) copy-start(bf16[128,24]{0,1:T(8,128)(2,1)} %get-tuple-element.173) | copy-start | bytes 18436
  60.6 4.0 %copy-start.32 = (s32[128]{0:T(128)S(1)}, s32[128]{0:T(128)}, u32[]{:S(2)}) copy-start(s32[128]{0:T(128)} %get-tuple-element.179) | copy-start | bytes 1540
  60.7 4.0 %copy-start.33 = (s32[128]{0:T(128)S(1)}, s32[128]{0:T(128)}, u32[]{:S(2)}) copy-start(s32[128]{0:T(128)} %get-tuple-element.180) | copy-start | bytes 1540
  60.7 4.2 %copy-start.2 = (bf16[1,128,128]{2,0,1:T(2,128)(2,1)S(1)}, bf16[1,128,128]{2,0,1:T(2,128)(2,1)}, u32[]{:S(2)}) copy-start(bf16[1,128,128]{2,0,1:T(2,128)(2,1)} %get-tuple-element.171) | copy-start | bytes 98308
  60.7 4.2 %copy-start.10 = (bf16[1,1,1,2,128,16]{4,5,3,2,1,0:T(8,128)(2,1)S(1)}, bf16[1,1,1,2,128,16]{4,5,3,2,1,0:T(8,128)(2,1)}, u32[]{:S(2)}) copy-start(bf16[1,1,1,2,128,16]{4,5,3,2,1,0:T(8,128)(2,1)} %get-tuple-element.149) | copy-start | bytes 24580
  60.7 4.3 %copy-start.6 = (s32[128,128]{1,0:T(8,128)S(1)}, s32[128,128]{1,0:T(8,128)}, u32[]{:S(2)}) copy-start(s32[128,128]{1,0:T(8,128)} %get-tuple-element.201) | copy-start | bytes 196612
  62.2 15.6 %copy-start.15 = (bf16[128,128]{1,0:T(8,128)(2,1)S(1)}, bf16[128,128]{1,0:T(8,128)(2,1)}, u32[]{:S(2)}) copy-start(bf16[128,128]{1,0:T(8,128)(2,1)} %get-tuple-element.124) | copy-start | bytes 98308
  62.2 15.6 %copy-start.16 = (bf16[128,128]{1,0:T(8,128)(2,1)S(1)}, bf16[128,128]{1,0:T(8,128)(2,1)}, u32[]{:S(2)}) copy-start(bf16[128,128]{1,0:T(8,128)(2,1)} %get-tuple-element.125) | copy-start | bytes 98308
  62.2 15.6 %copy-start.21 = (bf16[128,128]{1,0:T(8,128)(2,1)S(1)}, bf16[128,128]{1,0:T(8,128)(2,1)}, u32[]{:S(2)}) copy-start(bf16[128,128]{1,0:T(8,128)(2,1)} %get-tuple-element.126) | copy-start | bytes 98308
  62.3 15.6 %copy-start.22 = (bf16[128,128]{1,0:T(8,128)(2,1)S(1)}, bf16[128,128]{1,0:T(8,128)(2,1)}, u32[]{:S(2)}) copy-start(bf16[128,128]{1,0:T(8,128)(2,1)} %get-tuple-element.127) | copy-start | bytes 98308
  62.8 15.0 %collective-permute-start.1 = (bf16[2,128,1024]{2,1,0:T(8,128)(2,1)S(1)}, bf16[2,128,1024]{2,1,0:T(8,128)(2,1)S(1)}, u32[]{:S(2)}, u32[]{:S(2)}) collective-permute-start(bf16[2,128,1024]{2,1,0:T(8,128)(2,1)S(1)} %bitcast.233), channel_id=1, source_target_pairs={{0,4},{4,0},{8,12},{12,8},{16,20},{20,16},{24,28},{28,24},{32,36},... | collective-permute-start | bytes 1572872 | tf_op jit(solution)/shard_map/ppermute | solution.py:22
  77.8 2.6 %copy-start.3 = (bf16[1,128,128]{2,0,1:T(2,128)(2,1)S(1)}, bf16[1,128,128]{2,0,1:T(2,128)(2,1)}, u32[]{:S(2)}) copy-start(bf16[1,128,128]{2,0,1:T(2,128)(2,1)} %get-tuple-element.167) | copy-start | bytes 98308
  77.9 2.7 %copy-start.9 = (bf16[1,1,1,2,128,16]{4,5,3,2,1,0:T(8,128)(2,1)S(1)}, bf16[1,1,1,2,128,16]{4,5,3,2,1,0:T(8,128)(2,1)}, u32[]{:S(2)}) copy-start(bf16[1,1,1,2,128,16]{4,5,3,2,1,0:T(8,128)(2,1)} %get-tuple-element.148) | copy-start | bytes 24580
  77.9 2.8 %copy-start.30 = (s32[128]{0:T(128)S(1)}, s32[128]{0:T(128)}, u32[]{:S(2)}) copy-start(s32[128]{0:T(128)} %get-tuple-element.184) | copy-start | bytes 1540
  77.9 2.8 %copy-start.31 = (s32[128]{0:T(128)S(1)}, s32[128]{0:T(128)}, u32[]{:S(2)}) copy-start(s32[128]{0:T(128)} %get-tuple-element.191) | copy-start | bytes 1540
  77.9 2.9 %copy-start.5 = (s32[128,128]{1,0:T(8,128)S(1)}, s32[128,128]{1,0:T(8,128)}, u32[]{:S(2)}) copy-start(s32[128,128]{1,0:T(8,128)} %get-tuple-element.200) | copy-start | bytes 196612
  78.3 28.0 %copy-start.13 = (bf16[128,128]{1,0:T(8,128)(2,1)S(1)}, bf16[128,128]{1,0:T(8,128)(2,1)}, u32[]{:S(2)}) copy-start(bf16[128,128]{1,0:T(8,128)(2,1)} %get-tuple-element.120) | copy-start | bytes 98308
  78.4 28.0 %copy-start.14 = (bf16[128,128]{1,0:T(8,128)(2,1)S(1)}, bf16[128,128]{1,0:T(8,128)(2,1)}, u32[]{:S(2)}) copy-start(bf16[128,128]{1,0:T(8,128)(2,1)} %get-tuple-element.121) | copy-start | bytes 98308
  78.4 28.0 %copy-start.19 = (bf16[128,128]{1,0:T(8,128)(2,1)S(1)}, bf16[128,128]{1,0:T(8,128)(2,1)}, u32[]{:S(2)}) copy-start(bf16[128,128]{1,0:T(8,128)(2,1)} %get-tuple-element.122) | copy-start | bytes 98308
  78.4 28.0 %copy-start.20 = (bf16[128,128]{1,0:T(8,128)(2,1)S(1)}, bf16[128,128]{1,0:T(8,128)(2,1)}, u32[]{:S(2)}) copy-start(bf16[128,128]{1,0:T(8,128)(2,1)} %get-tuple-element.123) | copy-start | bytes 98308
  78.4 28.0 %collective-permute-start.2 = (bf16[2,128,1024]{2,1,0:T(8,128)(2,1)S(1)}, bf16[2,128,1024]{2,1,0:T(8,128)(2,1)S(1)}, u32[]{:S(2)}, u32[]{:S(2)}) collective-permute-start(bf16[2,128,1024]{2,1,0:T(8,128)(2,1)S(1)} %bitcast.247), channel_id=1, source_target_pairs={{0,8},{8,0},{4,12},{12,4},{16,24},{24,16},{20,28},{28,20},{32,40},... | collective-permute-start | bytes 1572872 | tf_op jit(solution)/shard_map/ppermute | solution.py:22
  106.4 3.5 %copy-start.29 = (s32[128]{0:T(128)S(1)}, s32[128]{0:T(128)}, u32[]{:S(2)}) copy-start(s32[128]{0:T(128)} %get-tuple-element.181) | copy-start | bytes 1540
  106.4 3.6 %copy-start.1 = (bf16[1,128,128]{2,0,1:T(2,128)(2,1)S(1)}, bf16[1,128,128]{2,0,1:T(2,128)(2,1)}, u32[]{:S(2)}) copy-start(bf16[1,128,128]{2,0,1:T(2,128)(2,1)} %get-tuple-element.163) | copy-start | bytes 98308
  106.4 3.6 %copy-start.8 = (bf16[1,1,1,2,128,16]{4,5,3,2,1,0:T(8,128)(2,1)S(1)}, bf16[1,1,1,2,128,16]{4,5,3,2,1,0:T(8,128)(2,1)}, u32[]{:S(2)}) copy-start(bf16[1,1,1,2,128,16]{4,5,3,2,1,0:T(8,128)(2,1)} %get-tuple-element.142) | copy-start | bytes 24580
  106.9 28.8 %copy-start.11 = (bf16[128,128]{1,0:T(8,128)(2,1)S(1)}, bf16[128,128]{1,0:T(8,128)(2,1)}, u32[]{:S(2)}) copy-start(bf16[128,128]{1,0:T(8,128)(2,1)} %get-tuple-element.116) | copy-start | bytes 98308
  106.9 28.8 %copy-start.12 = (bf16[128,128]{1,0:T(8,128)(2,1)S(1)}, bf16[128,128]{1,0:T(8,128)(2,1)}, u32[]{:S(2)}) copy-start(bf16[128,128]{1,0:T(8,128)(2,1)} %get-tuple-element.117) | copy-start | bytes 98308
  106.9 28.8 %copy-start.17 = (bf16[128,128]{1,0:T(8,128)(2,1)S(1)}, bf16[128,128]{1,0:T(8,128)(2,1)}, u32[]{:S(2)}) copy-start(bf16[128,128]{1,0:T(8,128)(2,1)} %get-tuple-element.118) | copy-start | bytes 98308
  106.9 28.8 %copy-start.18 = (bf16[128,128]{1,0:T(8,128)(2,1)S(1)}, bf16[128,128]{1,0:T(8,128)(2,1)}, u32[]{:S(2)}) copy-start(bf16[128,128]{1,0:T(8,128)(2,1)} %get-tuple-element.119) | copy-start | bytes 98308
  107.0 28.7 %collective-permute-start.3 = (bf16[2,128,1024]{2,1,0:T(8,128)(2,1)S(1)}, bf16[2,128,1024]{2,1,0:T(8,128)(2,1)S(1)}, u32[]{:S(2)}, u32[]{:S(2)}) collective-permute-start(bf16[2,128,1024]{2,1,0:T(8,128)(2,1)S(1)} %bitcast.248), channel_id=1, source_target_pairs={{0,16},{16,0},{4,20},{20,4},{8,24},{24,8},{12,28},{28,12},{32,48},... | collective-permute-start | bytes 1572872 | tf_op jit(solution)/shard_map/ppermute | solution.py:22
  135.8 2.4 %copy-start.7 = (bf16[1,1,1,2,128,16]{4,5,3,2,1,0:T(8,128)(2,1)S(1)}, bf16[1,1,1,2,128,16]{4,5,3,2,1,0:T(8,128)(2,1)}, u32[]{:S(2)}) copy-start(bf16[1,1,1,2,128,16]{4,5,3,2,1,0:T(8,128)(2,1)} %get-tuple-element.150) | copy-start | bytes 24580
  136.2 14.6 %collective-permute-start.4 = (bf16[2,128,1024]{2,1,0:T(8,128)(2,1)S(1)}, bf16[2,128,1024]{2,1,0:T(8,128)(2,1)S(1)}, u32[]{:S(2)}, u32[]{:S(2)}) collective-permute-start(bf16[2,128,1024]{2,1,0:T(8,128)(2,1)S(1)} %bitcast.249), channel_id=1, source_target_pairs={{0,32},{32,0},{4,36},{36,4},{8,40},{40,8},{12,44},{44,12},{16,48},... | collective-permute-start | bytes 1572872 | tf_op jit(solution)/shard_map/ppermute | solution.py:22
  151.4 27.8 %collective-permute-start.5 = (bf16[2,128,1024]{2,1,0:T(8,128)(2,1)S(1)}, bf16[2,128,1024]{2,1,0:T(8,128)(2,1)S(1)}, u32[]{:S(2)}, u32[]{:S(2)}) collective-permute-start(bf16[2,128,1024]{2,1,0:T(8,128)(2,1)S(1)} %bitcast.250), channel_id=1, source_target_pairs={{0,64},{64,0},{4,68},{68,4},{8,72},{72,8},{12,76},{76,12},{16,80},... | collective-permute-start | bytes 1572872 | tf_op jit(solution)/shard_map/ppermute | solution.py:22
where the time goes:
time: 181 us; the launch traced here: 180 us
  waiting for transfers between devices  103 us (57%)
  local copies, waits for them, and re-layouts  29.8 us (16%)
  starting transfers between devices  24.3 us (13%)
  matrix products  11.7 us (6%)
  other arithmetic  9.67 us (5%)
    ppermute x5, waiting for transfers between devices, from_partner(): return lax.ppermute(block, axis, route)  98.5 us
    unnamed x95, local copies, waits for them, and re-layouts  13.9 us
    ppermute x5, starting transfers between devices, from_partner(): return lax.ppermute(block, axis, route)  12.1 us
    ppermute x1, starting transfers between devices, from_behind(): return lax.ppermute(value, axis, pairs)  8.78 us
    all_to_all x1, waiting for transfers between devices, on_device(): lax.all_to_all(compressed, 'section', split_axis=2, concat_axis=1, tiled=...  4.89 us
    dot_general x10, matrix products, band_matrix(): jnp.einsum('sqt,tqc->sqc', coef_side, selector, preferred_element_type=jn...  4.58 us
  transfers between devices with their start and end apart: 7, of which 6 were waited for; matrix products, arithmetic and copies ran while one was open for 16% of the time, Pallas kernels for 0%

commit v1 on v0

--- a/solution.py
+++ b/solution.py
@@ -103,7 +103,19 @@
 
 def on_device(echoes, chirp, steer, pulse_order, band_coef, band_start, band_width):
     compressed = compress(echoes[:, 0], chirp)
-    pulse_rows = lax.all_to_all(compressed, "section", split_axis=2, concat_axis=1, tiled=True)
+    ways, here = (lax.axis_size("section"), lax.axis_index("section"))
+    width = compressed.shape[2] // ways
+    lengths = list(compressed.shape)
+    lengths[2] = width
+    height = lengths[1]
+    lengths[1] = height * ways
+    full = jnp.zeros(lengths, compressed.dtype)
+    for mask in range(ways):
+        part = lax.dynamic_slice_in_dim(compressed, (here ^ mask) * width, width, axis=2)
+        if mask:
+            part = lax.ppermute(part, "section", [(d, d ^ mask) for d in range(ways)])
+        full = lax.dynamic_update_slice_in_dim(full, part, (here ^ mask) * height, axis=1)
+    pulse_rows = full
     position_count = pulse_order.shape[1]
     positions = jnp.arange(position_count, dtype=jnp.int32)
     selector = (positions[:, None] == pulse_order[0][None, :]).astype(jnp.bfloat16)

time: 181 us -> 173 us (0.956)
  local copies, waits for them, and re-layouts: 29.8 us -> 18.9 us
  starting transfers between devices: 24.3 us -> 31 us
  waiting for transfers between devices: 103 us -> 99.6 us
    ppermute x0 -> x3, starting transfers between devices: none -> 9.76 us  [on_device(): part = lax.ppermute(part, 'section', [(d, d ^ mask) for d in range(ways)])]
    unnamed x95 -> x93, local copies, waits for them, and re-layouts: 13.9 us -> 4.97 us
    all_to_all x1 -> x0, waiting for transfers between devices: 4.89 us -> none  [on_device(): lax.all_to_all(compressed, 'section', split_axis=2, concat_axis=1, tiled=...]
    all_to_all x1 -> x0, starting transfers between devices: 3.49 us -> none  [on_device(): lax.all_to_all(compressed, 'section', split_axis=2, concat_axis=1, tiled=...]
  transfers between devices with their start and end apart: 7 -> 9, of which waited for: 6 -> 6; matrix products, arithmetic and copies ran while one was open for 16% -> 17% of each run, Pallas kernels for 0% -> 0%
where the time goes in v1:
time: 173 us; the launch traced here: 172 us
  waiting for transfers between devices  99.6 us (58%)
  starting transfers between devices  31 us (18%)
  local copies, waits for them, and re-layouts  18.9 us (11%)
  matrix products  11.7 us (7%)
  other arithmetic  9.65 us (6%)
    ppermute x5, waiting for transfers between devices, from_partner(): return lax.ppermute(block, axis, route)  98.8 us
    ppermute x5, starting transfers between devices, from_partner(): return lax.ppermute(block, axis, route)  12.5 us
    ppermute x3, starting transfers between devices, on_device(): part = lax.ppermute(part, 'section', [(d, d ^ mask) for d in range(ways)])  9.76 us
    ppermute x1, starting transfers between devices, from_behind(): return lax.ppermute(value, axis, pairs)  8.78 us
    unnamed x93, local copies, waits for them, and re-layouts  4.97 us
    dot_general x10, matrix products, band_matrix(): jnp.einsum('sqt,tqc->sqc', coef_side, selector, preferred_element_type=jn...  4.58 us
    dot_general x17, matrix products, add_piece(): jnp.einsum('pbi,io->pbo', window, table, preferred_element_type=jnp.float32)  3.56 us
  transfers between devices with their start and end apart: 9, of which 6 were waited for; matrix products, arithmetic and copies ran while one was open for 17% of the time, Pallas kernels for 0%

profile of v1, /device:TPU:1, one launch (start us, length us, event | category | flops | bytes accessed | tf_op | source)
XLA Modules:
  0.0 172.5 jit_solution(11453540824143393047)
XLA Ops:
  0.0 1.5 slice.435
  1.5 8.8 %collective-permute-start = (bf16[2,6,2048]{2,0,1:T(2,128)(2,1)}, bf16[2,6,2048]{2,0,1:T(2,128)(2,1)}, u32[]{:S(2)}, u32[]{:S(2)}) collective-permute-start(bf16[2,6,2048]{2,0,1:T(2,128)(2,1)} %slice.435), channel_id=1, source_target_pairs={{1,0},{2,1},{3,2},{5,4},{6,5},{7,6},{9,8},{10,9},{11,10},{13,12},{... | collective-permute-start | bytes 147464 | tf_op jit(solution)/shard_map/ppermute | solution.py:12
  10.3 0.7 maximum_maximum_fusion.1
  11.1 1.3 copy.144
  12.4 0.9 slice.436
  13.3 2.1 %reshape.578 = bf16[622336]{0:T(1024)(128)(2,1)S(1)} reshape(bf16[2,311168]{1,0:T(2,128)(2,1)S(1)} %slice.436) | data formatting | bytes 2489344
  15.5 2.2 %reshape.574 = bf16[2,128,2431]{2,1,0:T(8,128)(2,1)S(1)} reshape(bf16[622336]{0:T(1024)(128)(2,1)S(1)} %reshape.578) | data formatting | bytes 2489344 | tf_op jit(solution)/shard_map/reshape | solution.py:62
  17.6 1.1 slice.437
  18.7 1.7 copy.106
  20.6 0.9 fusion.186
  21.6 0.6 slice_bitcast_fusion.14
  22.2 0.6 slice_bitcast_fusion.35
  22.8 0.6 slice_bitcast_fusion.34
  23.4 0.6 fusion.197
  24.4 0.5 fusion.12
  24.9 0.6 fusion.195
  25.7 0.5 fusion.13
  26.1 0.7 fusion.207
  26.9 0.6 fusion.196
  27.8 0.5 fusion.10
  28.4 0.6 fusion.193
  29.2 0.5 fusion.11
  29.6 0.7 fusion.205
  30.3 0.6 fusion.194
  31.3 0.5 fusion.8
  31.9 0.6 fusion.191
  32.7 0.5 fusion.9
  33.1 0.7 fusion.203
  33.8 0.6 fusion.192
  34.5 0.8 iota_subtract_fusion.6
  35.2 1.4 maximum_maximum_fusion
  36.7 1.1 maximum_bitcast_fusion
  37.9 4.0 %while.14 = (s32[]{:T(128)}, f32[6,32,256]{2,1,0:T(8,128)S(1)}, bf16[6,48,256]{2,1,0:T(8,128)(2,1)S(1)}, bf16[17,256,256]{2,1,0:T(8,128)(2,1)S(1)}, s32[]{:T(128)}, /*index=5*/s32[]{:T(128)}) while((s32[]{:T(128)}, f32[6,32,256]{2,1,0:T(8,128)S(1)}, bf16[6,48,256]{2,1,0:T(8,128)(2,1)S(1)}, bf16[17,256,256]{2,1,0:T(8,128)(2,1)S(1)}, ...), condition=%wide.region_1.2_spmd.clone, body=%wide.region_0.1_spmd.clone.sunk | while | flops 25264132 | bytes 623695 | solution.py:93
  38.0 0.2 convolution_add_fusion.2
  38.4 0.2 convolution_add_fusion.2
  38.7 0.2 convolution_add_fusion.2
  38.9 0.2 convolution_add_fusion.2
  42.1 1.9 %collective-permute-start.1 = (bf16[2,6,1024]{2,0,1:T(2,128)(2,1)S(1)}, bf16[2,6,1024]{2,0,1:T(2,128)(2,1)S(1)}, u32[]{:S(2)}, u32[]{:S(2)}) collective-permute-start(bf16[2,6,1024]{2,0,1:T(2,128)(2,1)S(1)} %get-tuple-element.144), channel_id=1, source_target_pairs={{0,128},{128,0},{256,384},{384,256},{1,129},{129,1},{257,385},{385... | collective-permute-start | bytes 73736 | tf_op jit(solution)/shard_map/ppermute | solution.py:116
  44.0 2.1 %collective-permute-start.2 = (bf16[2,6,1024]{2,0,1:T(2,128)(2,1)S(1)}, bf16[2,6,1024]{2,0,1:T(2,128)(2,1)S(1)}, u32[]{:S(2)}, u32[]{:S(2)}) collective-permute-start(bf16[2,6,1024]{2,0,1:T(2,128)(2,1)S(1)} %get-tuple-element.143), channel_id=1, source_target_pairs={{0,256},{128,384},{256,0},{384,128},{1,257},{129,385},{257,1},{385... | collective-permute-start | bytes 73736 | tf_op jit(solution)/shard_map/ppermute | solution.py:116
  46.1 5.7 %collective-permute-start.3 = (bf16[2,6,1024]{2,0,1:T(2,128)(2,1)S(1)}, bf16[2,6,1024]{2,0,1:T(2,128)(2,1)S(1)}, u32[]{:S(2)}, u32[]{:S(2)}) collective-permute-start(bf16[2,6,1024]{2,0,1:T(2,128)(2,1)S(1)} %get-tuple-element.142), channel_id=1, source_target_pairs={{0,384},{128,256},{256,128},{384,0},{1,385},{129,257},{257,129},{3... | collective-permute-start | bytes 73736 | tf_op jit(solution)/shard_map/ppermute | solution.py:116
  52.0 0.2 dynamic_update_slice.12
  52.3 0.2 dynamic_update_slice.13
  52.5 0.2 dynamic_update_slice.14
  52.8 0.8 collective-permute-done.3
  53.8 0.3 convolution_convert_fusion.5
  54.1 1.9 %collective-permute-start.4 = (bf16[2,128,1024]{2,1,0:T(8,128)(2,1)S(1)}, bf16[2,128,1024]{2,1,0:T(8,128)(2,1)S(1)}, u32[]{:S(2)}, u32[]{:S(2)}) collective-permute-start(bf16[2,128,1024]{2,1,0:T(8,128)(2,1)S(1)} %bitcast.234), channel_id=1, source_target_pairs={{0,4},{4,0},{8,12},{12,8},{16,20},{20,16},{24,28},{28,24},{32,36},... | collective-permute-start | bytes 1572872 | tf_op jit(solution)/shard_map/ppermute | solution.py:22
  56.3 0.5 fusion.6
  56.9 12.1 %collective-permute-done.4 = bf16[2,128,1024]{2,1,0:T(8,128)(2,1)S(1)} collective-permute-done((bf16[2,128,1024]{2,1,0:T(8,128)(2,1)S(1)}, bf16[2,128,1024]{2,1,0:T(8,128)(2,1)S(1)}, u32[]{:S(2)}, u32[]{:S(2)}) %collective-permute-start.4) | collective-permute-done | bytes 524320 | tf_op jit(solution)/shard_map/ppermute | solution.py:22
  69.1 0.5 convolution_convert_fusion.4
  69.6 2.1 %collective-permute-start.5 = (bf16[2,128,1024]{2,1,0:T(8,128)(2,1)S(1)}, bf16[2,128,1024]{2,1,0:T(8,128)(2,1)S(1)}, u32[]{:S(2)}, u32[]{:S(2)}) collective-permute-start(bf16[2,128,1024]{2,1,0:T(8,128)(2,1)S(1)} %bitcast.247), channel_id=1, source_target_pairs={{0,8},{8,0},{4,12},{12,4},{16,24},{24,16},{20,28},{28,20},{32,40},... | collective-permute-start | bytes 1572872 | tf_op jit(solution)/shard_map/ppermute | solution.py:22
  72.0 0.5 fusion.7
  72.4 25.1 %collective-permute-done.5 = bf16[2,128,1024]{2,1,0:T(8,128)(2,1)S(1)} collective-permute-done((bf16[2,128,1024]{2,1,0:T(8,128)(2,1)S(1)}, bf16[2,128,1024]{2,1,0:T(8,128)(2,1)S(1)}, u32[]{:S(2)}, u32[]{:S(2)}) %collective-permute-start.5) | collective-permute-done | bytes 524320 | tf_op jit(solution)/shard_map/ppermute | solution.py:22
  97.7 0.5 convolution_convert_fusion.3
  98.2 3.5 %collective-permute-start.6 = (bf16[2,128,1024]{2,1,0:T(8,128)(2,1)S(1)}, bf16[2,128,1024]{2,1,0:T(8,128)(2,1)S(1)}, u32[]{:S(2)}, u32[]{:S(2)}) collective-permute-start(bf16[2,128,1024]{2,1,0:T(8,128)(2,1)S(1)} %bitcast.248), channel_id=1, source_target_pairs={{0,16},{16,0},{4,20},{20,4},{8,24},{24,8},{12,28},{28,12},{32,48},... | collective-permute-start | bytes 1572872 | tf_op jit(solution)/shard_map/ppermute | solution.py:22
  102.1 0.5 fusion.4
  102.6 25.0 %collective-permute-done.6 = bf16[2,128,1024]{2,1,0:T(8,128)(2,1)S(1)} collective-permute-done((bf16[2,128,1024]{2,1,0:T(8,128)(2,1)S(1)}, bf16[2,128,1024]{2,1,0:T(8,128)(2,1)S(1)}, u32[]{:S(2)}, u32[]{:S(2)}) %collective-permute-start.6) | collective-permute-done | bytes 524320 | tf_op jit(solution)/shard_map/ppermute | solution.py:22
  127.7 0.5 convolution_convert_fusion.2
  128.1 1.9 %collective-permute-start.7 = (bf16[2,128,1024]{2,1,0:T(8,128)(2,1)S(1)}, bf16[2,128,1024]{2,1,0:T(8,128)(2,1)S(1)}, u32[]{:S(2)}, u32[]{:S(2)}) collective-permute-start(bf16[2,128,1024]{2,1,0:T(8,128)(2,1)S(1)} %bitcast.249), channel_id=1, source_target_pairs={{0,32},{32,0},{4,36},{36,4},{8,40},{40,8},{12,44},{44,12},{16,48},... | collective-permute-start | bytes 1572872 | tf_op jit(solution)/shard_map/ppermute | solution.py:22
  130.3 0.5 fusion.5
  130.8 12.2 %collective-permute-done.7 = bf16[2,128,1024]{2,1,0:T(8,128)(2,1)S(1)} collective-permute-done((bf16[2,128,1024]{2,1,0:T(8,128)(2,1)S(1)}, bf16[2,128,1024]{2,1,0:T(8,128)(2,1)S(1)}, u32[]{:S(2)}, u32[]{:S(2)}) %collective-permute-start.7) | collective-permute-done | bytes 524320 | tf_op jit(solution)/shard_map/ppermute | solution.py:22
  143.1 0.5 convolution_convert_fusion.1
  143.5 3.0 %collective-permute-start.8 = (bf16[2,128,1024]{2,1,0:T(8,128)(2,1)S(1)}, bf16[2,128,1024]{2,1,0:T(8,128)(2,1)S(1)}, u32[]{:S(2)}, u32[]{:S(2)}) collective-permute-start(bf16[2,128,1024]{2,1,0:T(8,128)(2,1)S(1)} %bitcast.250), channel_id=1, source_target_pairs={{0,64},{64,0},{4,68},{68,4},{8,72},{72,8},{12,76},{76,12},{16,80},... | collective-permute-start | bytes 1572872 | tf_op jit(solution)/shard_map/ppermute | solution.py:22
  146.7 24.4 %collective-permute-done.8 = bf16[2,128,1024]{2,1,0:T(8,128)(2,1)S(1)} collective-permute-done((bf16[2,128,1024]{2,1,0:T(8,128)(2,1)S(1)}, bf16[2,128,1024]{2,1,0:T(8,128)(2,1)S(1)}, u32[]{:S(2)}, u32[]{:S(2)}) %collective-permute-start.8) | collective-permute-done | bytes 524320 | tf_op jit(solution)/shard_map/ppermute | solution.py:22
  171.2 1.2 convolution_convert_fusion
  (151 shorter events, 6.9 us)
Async XLA Ops:
  0.0 21.4 %copy-start = (bf16[2,1,128,24]{2,3,1,0:T(8,128)(2,1)S(1)}, bf16[2,1,128,24]{2,3,1,0:T(8,128)(2,1)}, u32[]{:S(2)}) copy-start(bf16[2,1,128,24]{2,3,1,0:T(8,128)(2,1)} %param.11) | copy-start | bytes 36868
  1.5 35.3 %collective-permute-start = (bf16[2,6,2048]{2,0,1:T(2,128)(2,1)}, bf16[2,6,2048]{2,0,1:T(2,128)(2,1)}, u32[]{:S(2)}, u32[]{:S(2)}) collective-permute-start(bf16[2,6,2048]{2,0,1:T(2,128)(2,1)} %slice.435), channel_id=1, source_target_pairs={{1,0},{2,1},{3,2},{5,4},{6,5},{7,6},{9,8},{10,9},{11,10},{13,12},{... | collective-permute-start | bytes 147464 | tf_op jit(solution)/shard_map/ppermute | solution.py:12
  20.4 1.1 copy-start.34
  20.4 1.8 %copy-start.27 = (s32[5,1,2,128]{3,2,1,0:T(2,128)S(1)}, s32[5,1,2,128]{3,2,1,0:T(2,128)}, u32[]{:S(2)}) copy-start(s32[5,1,2,128]{3,2,1,0:T(2,128)} %param.14) | copy-start | bytes 15364
  20.4 2.4 %copy-start.28 = (s32[5,1,2,128]{3,2,1,0:T(2,128)S(1)}, s32[5,1,2,128]{3,2,1,0:T(2,128)}, u32[]{:S(2)}) copy-start(s32[5,1,2,128]{3,2,1,0:T(2,128)} %param.15) | copy-start | bytes 15364
  20.4 3.0 %copy-start.4 = (bf16[5,1,2,2,128,16]{4,5,3,2,1,0:T(8,128)(2,1)S(1)}, bf16[5,1,2,2,128,16]{4,5,3,2,1,0:T(8,128)(2,1)}, u32[]{:S(2)}) copy-start(bf16[5,1,2,2,128,16]{4,5,3,2,1,0:T(8,128)(2,1)} %param.13) | copy-start | bytes 245764
  21.6 2.4 %copy-start.23 = (bf16[2,128,24]{1,2,0:T(8,128)(2,1)}, bf16[2,128,24]{1,2,0:T(8,128)(2,1)S(1)}, u32[]{:S(2)}) copy-start(bf16[2,128,24]{1,2,0:T(8,128)(2,1)S(1)} %fusion.14) | copy-start | bytes 36868
  37.8 14.1 %copy-start.24 = (bf16[2,128,24]{1,2,0:T(8,128)(2,1)S(1)}, bf16[2,128,24]{1,2,0:T(8,128)(2,1)}, u32[]{:S(2)}) copy-start(bf16[2,128,24]{1,2,0:T(8,128)(2,1)} %copy-done.23) | copy-start | bytes 36868
  37.9 15.8 %copy-start.25 = (bf16[128,24]{0,1:T(8,128)(2,1)S(1)}, bf16[128,24]{0,1:T(8,128)(2,1)}, u32[]{:S(2)}) copy-start(bf16[128,24]{0,1:T(8,128)(2,1)} %get-tuple-element.176) | copy-start | bytes 18436
  37.9 15.8 %copy-start.26 = (bf16[128,24]{0,1:T(8,128)(2,1)S(1)}, bf16[128,24]{0,1:T(8,128)(2,1)}, u32[]{:S(2)}) copy-start(bf16[128,24]{0,1:T(8,128)(2,1)} %get-tuple-element.177) | copy-start | bytes 18436
  37.9 18.2 %copy-start.3 = (bf16[1,128,128]{2,0,1:T(2,128)(2,1)S(1)}, bf16[1,128,128]{2,0,1:T(2,128)(2,1)}, u32[]{:S(2)}) copy-start(bf16[1,128,128]{2,0,1:T(2,128)(2,1)} %get-tuple-element.175) | copy-start | bytes 98308
  41.9 14.1 %copy-start.32 = (s32[128]{0:T(128)S(1)}, s32[128]{0:T(128)}, u32[]{:S(2)}) copy-start(s32[128]{0:T(128)} %get-tuple-element.183) | copy-start | bytes 1540
  41.9 14.1 %copy-start.33 = (s32[128]{0:T(128)S(1)}, s32[128]{0:T(128)}, u32[]{:S(2)}) copy-start(s32[128]{0:T(128)} %get-tuple-element.184) | copy-start | bytes 1540
  41.9 14.3 %copy-start.10 = (bf16[1,1,1,2,128,16]{4,5,3,2,1,0:T(8,128)(2,1)S(1)}, bf16[1,1,1,2,128,16]{4,5,3,2,1,0:T(8,128)(2,1)}, u32[]{:S(2)}) copy-start(bf16[1,1,1,2,128,16]{4,5,3,2,1,0:T(8,128)(2,1)} %get-tuple-element.153) | copy-start | bytes 24580
  42.0 14.4 %copy-start.6 = (s32[128,128]{1,0:T(8,128)S(1)}, s32[128,128]{1,0:T(8,128)}, u32[]{:S(2)}) copy-start(s32[128,128]{1,0:T(8,128)} %get-tuple-element.205) | copy-start | bytes 196612
  42.1 10.1 %collective-permute-start.1 = (bf16[2,6,1024]{2,0,1:T(2,128)(2,1)S(1)}, bf16[2,6,1024]{2,0,1:T(2,128)(2,1)S(1)}, u32[]{:S(2)}, u32[]{:S(2)}) collective-permute-start(bf16[2,6,1024]{2,0,1:T(2,128)(2,1)S(1)} %get-tuple-element.144), channel_id=1, source_target_pairs={{0,128},{128,0},{256,384},{384,256},{1,129},{129,1},{257,385},{385... | collective-permute-start | bytes 73736 | tf_op jit(solution)/shard_map/ppermute | solution.py:116
  44.0 8.5 %collective-permute-start.2 = (bf16[2,6,1024]{2,0,1:T(2,128)(2,1)S(1)}, bf16[2,6,1024]{2,0,1:T(2,128)(2,1)S(1)}, u32[]{:S(2)}, u32[]{:S(2)}) collective-permute-start(bf16[2,6,1024]{2,0,1:T(2,128)(2,1)S(1)} %get-tuple-element.143), channel_id=1, source_target_pairs={{0,256},{128,384},{256,0},{384,128},{1,257},{129,385},{257,1},{385... | collective-permute-start | bytes 73736 | tf_op jit(solution)/shard_map/ppermute | solution.py:116
  46.1 7.4 %collective-permute-start.3 = (bf16[2,6,1024]{2,0,1:T(2,128)(2,1)S(1)}, bf16[2,6,1024]{2,0,1:T(2,128)(2,1)S(1)}, u32[]{:S(2)}, u32[]{:S(2)}) collective-permute-start(bf16[2,6,1024]{2,0,1:T(2,128)(2,1)S(1)} %get-tuple-element.142), channel_id=1, source_target_pairs={{0,384},{128,256},{256,128},{384,0},{1,385},{129,257},{257,129},{3... | collective-permute-start | bytes 73736 | tf_op jit(solution)/shard_map/ppermute | solution.py:116
  52.0 17.0 %copy-start.15 = (bf16[128,128]{1,0:T(8,128)(2,1)S(1)}, bf16[128,128]{1,0:T(8,128)(2,1)}, u32[]{:S(2)}) copy-start(bf16[128,128]{1,0:T(8,128)(2,1)} %get-tuple-element.124) | copy-start | bytes 98308
  52.0 17.0 %copy-start.16 = (bf16[128,128]{1,0:T(8,128)(2,1)S(1)}, bf16[128,128]{1,0:T(8,128)(2,1)}, u32[]{:S(2)}) copy-start(bf16[128,128]{1,0:T(8,128)(2,1)} %get-tuple-element.125) | copy-start | bytes 98308
  52.0 17.0 %copy-start.21 = (bf16[128,128]{1,0:T(8,128)(2,1)S(1)}, bf16[128,128]{1,0:T(8,128)(2,1)}, u32[]{:S(2)}) copy-start(bf16[128,128]{1,0:T(8,128)(2,1)} %get-tuple-element.126) | copy-start | bytes 98308
  52.0 17.0 %copy-start.22 = (bf16[128,128]{1,0:T(8,128)(2,1)S(1)}, bf16[128,128]{1,0:T(8,128)(2,1)}, u32[]{:S(2)}) copy-start(bf16[128,128]{1,0:T(8,128)(2,1)} %get-tuple-element.127) | copy-start | bytes 98308
  54.1 14.9 %collective-permute-start.4 = (bf16[2,128,1024]{2,1,0:T(8,128)(2,1)S(1)}, bf16[2,128,1024]{2,1,0:T(8,128)(2,1)S(1)}, u32[]{:S(2)}, u32[]{:S(2)}) collective-permute-start(bf16[2,128,1024]{2,1,0:T(8,128)(2,1)S(1)} %bitcast.234), channel_id=1, source_target_pairs={{0,4},{4,0},{8,12},{12,8},{16,20},{20,16},{24,28},{28,24},{32,36},... | collective-permute-start | bytes 1572872 | tf_op jit(solution)/shard_map/ppermute | solution.py:22
  69.0 2.6 %copy-start.2 = (bf16[1,128,128]{2,0,1:T(2,128)(2,1)S(1)}, bf16[1,128,128]{2,0,1:T(2,128)(2,1)}, u32[]{:S(2)}) copy-start(bf16[1,128,128]{2,0,1:T(2,128)(2,1)} %get-tuple-element.171) | copy-start | bytes 98308
  69.1 2.7 %copy-start.9 = (bf16[1,1,1,2,128,16]{4,5,3,2,1,0:T(8,128)(2,1)S(1)}, bf16[1,1,1,2,128,16]{4,5,3,2,1,0:T(8,128)(2,1)}, u32[]{:S(2)}) copy-start(bf16[1,1,1,2,128,16]{4,5,3,2,1,0:T(8,128)(2,1)} %get-tuple-element.152) | copy-start | bytes 24580
  69.1 2.8 %copy-start.30 = (s32[128]{0:T(128)S(1)}, s32[128]{0:T(128)}, u32[]{:S(2)}) copy-start(s32[128]{0:T(128)} %get-tuple-element.188) | copy-start | bytes 1540
  69.1 2.8 %copy-start.31 = (s32[128]{0:T(128)S(1)}, s32[128]{0:T(128)}, u32[]{:S(2)}) copy-start(s32[128]{0:T(128)} %get-tuple-element.195) | copy-start | bytes 1540
  69.1 2.9 %copy-start.5 = (s32[128,128]{1,0:T(8,128)S(1)}, s32[128,128]{1,0:T(8,128)}, u32[]{:S(2)}) copy-start(s32[128,128]{1,0:T(8,128)} %get-tuple-element.204) | copy-start | bytes 196612
  69.6 28.0 %copy-start.13 = (bf16[128,128]{1,0:T(8,128)(2,1)S(1)}, bf16[128,128]{1,0:T(8,128)(2,1)}, u32[]{:S(2)}) copy-start(bf16[128,128]{1,0:T(8,128)(2,1)} %get-tuple-element.120) | copy-start | bytes 98308
  69.6 28.0 %copy-start.14 = (bf16[128,128]{1,0:T(8,128)(2,1)S(1)}, bf16[128,128]{1,0:T(8,128)(2,1)}, u32[]{:S(2)}) copy-start(bf16[128,128]{1,0:T(8,128)(2,1)} %get-tuple-element.121) | copy-start | bytes 98308
  69.6 28.0 %copy-start.19 = (bf16[128,128]{1,0:T(8,128)(2,1)S(1)}, bf16[128,128]{1,0:T(8,128)(2,1)}, u32[]{:S(2)}) copy-start(bf16[128,128]{1,0:T(8,128)(2,1)} %get-tuple-element.122) | copy-start | bytes 98308
  69.6 28.0 %copy-start.20 = (bf16[128,128]{1,0:T(8,128)(2,1)S(1)}, bf16[128,128]{1,0:T(8,128)(2,1)}, u32[]{:S(2)}) copy-start(bf16[128,128]{1,0:T(8,128)(2,1)} %get-tuple-element.123) | copy-start | bytes 98308
  69.6 28.0 %collective-permute-start.5 = (bf16[2,128,1024]{2,1,0:T(8,128)(2,1)S(1)}, bf16[2,128,1024]{2,1,0:T(8,128)(2,1)S(1)}, u32[]{:S(2)}, u32[]{:S(2)}) collective-permute-start(bf16[2,128,1024]{2,1,0:T(8,128)(2,1)S(1)} %bitcast.247), channel_id=1, source_target_pairs={{0,8},{8,0},{4,12},{12,4},{16,24},{24,16},{20,28},{28,20},{32,40},... | collective-permute-start | bytes 1572872 | tf_op jit(solution)/shard_map/ppermute | solution.py:22
  97.6 4.1 %copy-start.29 = (s32[128]{0:T(128)S(1)}, s32[128]{0:T(128)}, u32[]{:S(2)}) copy-start(s32[128]{0:T(128)} %get-tuple-element.185) | copy-start | bytes 1540
  97.6 4.2 %copy-start.1 = (bf16[1,128,128]{2,0,1:T(2,128)(2,1)S(1)}, bf16[1,128,128]{2,0,1:T(2,128)(2,1)}, u32[]{:S(2)}) copy-start(bf16[1,128,128]{2,0,1:T(2,128)(2,1)} %get-tuple-element.167) | copy-start | bytes 98308
  97.6 4.2 %copy-start.8 = (bf16[1,1,1,2,128,16]{4,5,3,2,1,0:T(8,128)(2,1)S(1)}, bf16[1,1,1,2,128,16]{4,5,3,2,1,0:T(8,128)(2,1)}, u32[]{:S(2)}) copy-start(bf16[1,1,1,2,128,16]{4,5,3,2,1,0:T(8,128)(2,1)} %get-tuple-element.146) | copy-start | bytes 24580
  98.1 29.5 %copy-start.11 = (bf16[128,128]{1,0:T(8,128)(2,1)S(1)}, bf16[128,128]{1,0:T(8,128)(2,1)}, u32[]{:S(2)}) copy-start(bf16[128,128]{1,0:T(8,128)(2,1)} %get-tuple-element.116) | copy-start | bytes 98308
  98.1 29.5 %copy-start.12 = (bf16[128,128]{1,0:T(8,128)(2,1)S(1)}, bf16[128,128]{1,0:T(8,128)(2,1)}, u32[]{:S(2)}) copy-start(bf16[128,128]{1,0:T(8,128)(2,1)} %get-tuple-element.117) | copy-start | bytes 98308
  98.1 29.5 %copy-start.17 = (bf16[128,128]{1,0:T(8,128)(2,1)S(1)}, bf16[128,128]{1,0:T(8,128)(2,1)}, u32[]{:S(2)}) copy-start(bf16[128,128]{1,0:T(8,128)(2,1)} %get-tuple-element.118) | copy-start | bytes 98308
  98.1 29.5 %copy-start.18 = (bf16[128,128]{1,0:T(8,128)(2,1)S(1)}, bf16[128,128]{1,0:T(8,128)(2,1)}, u32[]{:S(2)}) copy-start(bf16[128,128]{1,0:T(8,128)(2,1)} %get-tuple-element.119) | copy-start | bytes 98308
  98.2 29.4 %collective-permute-start.6 = (bf16[2,128,1024]{2,1,0:T(8,128)(2,1)S(1)}, bf16[2,128,1024]{2,1,0:T(8,128)(2,1)S(1)}, u32[]{:S(2)}, u32[]{:S(2)}) collective-permute-start(bf16[2,128,1024]{2,1,0:T(8,128)(2,1)S(1)} %bitcast.248), channel_id=1, source_target_pairs={{0,16},{16,0},{4,20},{20,4},{8,24},{24,8},{12,28},{28,12},{32,48},... | collective-permute-start | bytes 1572872 | tf_op jit(solution)/shard_map/ppermute | solution.py:22
  127.7 2.5 %copy-start.7 = (bf16[1,1,1,2,128,16]{4,5,3,2,1,0:T(8,128)(2,1)S(1)}, bf16[1,1,1,2,128,16]{4,5,3,2,1,0:T(8,128)(2,1)}, u32[]{:S(2)}) copy-start(bf16[1,1,1,2,128,16]{4,5,3,2,1,0:T(8,128)(2,1)} %get-tuple-element.154) | copy-start | bytes 24580
  128.1 14.9 %collective-permute-start.7 = (bf16[2,128,1024]{2,1,0:T(8,128)(2,1)S(1)}, bf16[2,128,1024]{2,1,0:T(8,128)(2,1)S(1)}, u32[]{:S(2)}, u32[]{:S(2)}) collective-permute-start(bf16[2,128,1024]{2,1,0:T(8,128)(2,1)S(1)} %bitcast.249), channel_id=1, source_target_pairs={{0,32},{32,0},{4,36},{36,4},{8,40},{40,8},{12,44},{44,12},{16,48},... | collective-permute-start | bytes 1572872 | tf_op jit(solution)/shard_map/ppermute | solution.py:22
  143.5 27.7 %collective-permute-start.8 = (bf16[2,128,1024]{2,1,0:T(8,128)(2,1)S(1)}, bf16[2,128,1024]{2,1,0:T(8,128)(2,1)S(1)}, u32[]{:S(2)}, u32[]{:S(2)}) collective-permute-start(bf16[2,128,1024]{2,1,0:T(8,128)(2,1)S(1)} %bitcast.250), channel_id=1, source_target_pairs={{0,64},{64,0},{4,68},{68,4},{8,72},{72,8},{12,76},{76,12},{16,80},... | collective-permute-start | bytes 1572872 | tf_op jit(solution)/shard_map/ppermute | solution.py:22
